TPU v7x, 512 devices: a whole 4x8x8 slice. The times are simulated.
512 devices in a mesh: head: 8 (over z), blk: 64 (over x, y, core).
Axes of the slice: x: 4, y: 8, z: 8, core: 2. Of those that a mesh axis runs over, the one named last changes fastest.
Arguments:
- vision: bfloat16 [4, 1408, 8192], P(None, 'head', 'blk'), may hold values from -600 to 600
- ln_gain: float32 [1408], P('head'), may hold values from 0.5 to 1.5
- merge_proj: bfloat16 [4, 1408, 1408], P(None, 'head'), may hold values from -0.078125 to 0.078125
- image_slot: int32 [2048], P('blk'), may hold values from 0 to 32764, as said below
- text: bfloat16 [1408, 32768], P('head', 'blk'), may hold values from -600 to 600
- rms_gain: float32 [1408], replicated, may hold values from 0.5 to 1.5
- wqkv: bfloat16 [3, 1408, 1408], P(None, 'head'), may hold values from -0.31835938 to 0.31835938
- pcache: bfloat16 [2, 1408, 131072], P(None, 'head', 'blk'), may hold values from -300 to 300
- block_table: int32 [64, 128], replicated, may hold values from -1 to 4095, as said below
- cache_len: int32 [64], P('blk'), may hold values from 1 to 4096, as said below
Outputs:
- attended: bfloat16 [1408, 32768], P('head', 'blk')
- new_cache: bfloat16 [2, 1408, 32768], P(None, 'head', 'blk')
Inputs may be any that keep to these rules, and one draw needn't show every extreme that they name: `image_slot`: pieces never intersect and start at multiples of 4; the 32 pieces held by one index of blk start in the rows of 32 different requests, and every request receives exactly 32 pieces. `block_table`: row r holds a block number for j < ceil(cache_len[r] / 32) and -1 after; no block number appears twice; index d of blk holds blocks d * 64 to (d+1) * 64 - 1. The longest request has exactly 2 blocks on every index of blk; every other request has at most one block on any index. `cache_len`: exactly one request, the longest, has 4096 cached positions; all others have fewer.
All inputs are finite; a program needn't handle non-finite values.
Results may differ from a plain program's by a relative error of at most 0.025.
The roundings to bfloat16 on the way count: a program that leaves them out, or rounds other values in their place, can miss the bound.
Values may be sent and summed in bfloat16 or wider, within the bound.
A program may use at most 128 MiB of HBM per device.

v0:
```python
import math
import jax
import jax.numpy as jnp
from jax import lax
from jax.sharding import PartitionSpec as P

D = 1408
HD = 88
BS = 32
masked_score = -1e30


def rotary_columns(values, places):
    half = values.shape[1] // 2
    freq_index = jnp.arange(half, dtype=jnp.float32)
    inverse = jnp.exp(freq_index * (-2.0 * math.log(10000.0) / values.shape[1]))
    angles = inverse[:, None] * places[None, :]
    cosine = jnp.cos(angles)[None]
    sine_part = jnp.sin(angles)[None]
    leading = values[:, :half]
    trailing = values[:, half:]
    return jnp.concatenate(
        [leading * cosine - trailing * sine_part, trailing * cosine + leading * sine_part], axis=1
    )


def softmax_part(query_block, keys, values, mask, scale):
    scores = (
        jnp.einsum("hdq,hdk->hqk", query_block, keys, preferred_element_type=jnp.float32) * scale
    )
    scores = jnp.where(mask[None], scores, masked_score)
    highest = jnp.max(scores, axis=2)
    expo = jnp.where(mask[None], jnp.exp(scores - highest[:, :, None]), 0.0)
    total = jnp.sum(expo, axis=2)
    mixed = jnp.einsum("hqk,hdk->hdq", expo, values, precision=lax.Precision.HIGHEST)
    return (mixed, highest, total)


def fold_softmax(first, second):
    mixed_a, high_a, total_a = first
    mixed_b, high_b, total_b = second
    top = jnp.maximum(high_a, high_b)
    factor_a = jnp.exp(high_a - top)
    factor_b = jnp.exp(high_b - top)
    return (
        mixed_a * factor_a[:, None, :] + mixed_b * factor_b[:, None, :],
        top,
        total_a * factor_a + total_b * factor_b,
    )


def unblock(parts):
    mixed, highest, total = parts
    heads_here = mixed.shape[1]
    mixed = jnp.transpose(mixed, (1, 2, 0, 3)).reshape(heads_here, mixed.shape[2], -1)
    highest = jnp.transpose(highest, (1, 0, 2)).reshape(heads_here, -1)
    total = jnp.transpose(total, (1, 0, 2)).reshape(heads_here, -1)
    return (mixed, highest, total)


def shards(
    vision, ln_gain, merge_proj, image_slot, text, rms_gain, wqkv, pcache, block_table, cache_len
):
    local = vision.shape[1]
    groups = vision.shape[2]
    floats = vision.astype(jnp.float32)
    totals, squares = lax.psum((jnp.sum(floats, axis=1), jnp.sum(floats * floats, axis=1)), "head")
    average = totals / D
    spread = squares / D - average * average
    normed_vision = (
        (floats - average[:, None, :])
        * lax.rsqrt(spread + 1e-06)[:, None, :]
        * ln_gain[None, :, None]
    ).astype(jnp.bfloat16)
    partial_rows = jnp.einsum(
        "tcd,tcg->dg", merge_proj, normed_vision, preferred_element_type=jnp.float32
    )
    merged_columns = lax.psum_scatter(partial_rows, "head", scatter_dimension=0, tiled=True).astype(
        jnp.bfloat16
    )
    merged = jnp.transpose(merged_columns)
    devices = lax.axis_size("blk")
    here = lax.axis_index("blk")
    rows_here = text.shape[1]
    pieces = image_slot.shape[0]
    piece_rows = groups // pieces
    lines = jnp.arange(rows_here, dtype=jnp.int32)
    offsets = jnp.arange(piece_rows, dtype=jnp.int32)
    target = image_slot // rows_here
    within = image_slot % rows_here
    select = target[None, :] == jnp.arange(devices, dtype=jnp.int32)[:, None]
    outbound = (
        jnp.dot(
            select.astype(jnp.bfloat16),
            merged.reshape(pieces, piece_rows * local),
            preferred_element_type=jnp.float32,
        )
        .astype(jnp.bfloat16)
        .reshape(devices, piece_rows, local)
    )
    starts = jnp.sum(jnp.where(select, within[None, :] + 1, 0), axis=1) - 1
    arrived, arrived_start = (
        lax.all_to_all(outbound, "blk", split_axis=0, concat_axis=0, tiled=True),
        lax.all_to_all(starts, "blk", split_axis=0, concat_axis=0, tiled=True),
    )
    row_ids = (arrived_start[:, None] + offsets[None, :]).reshape(-1)
    present = jnp.repeat(arrived_start >= 0, piece_rows)
    hits = (row_ids[:, None] == lines[None, :]) & present[:, None]
    placed_rows = jnp.einsum(
        "kl,kr->lr",
        arrived.reshape(devices * piece_rows, local),
        hits.astype(jnp.bfloat16),
        preferred_element_type=jnp.float32,
    ).astype(jnp.bfloat16)
    covered = jnp.any(hits, axis=0)
    placed = jnp.where(covered[None, :], placed_rows, text)
    row_floats = placed.astype(jnp.float32)
    square_sums = lax.psum(jnp.sum(row_floats * row_floats, axis=0), "head")
    gain_here = lax.dynamic_slice_in_dim(rms_gain, lax.axis_index("head") * local, local)
    normed = (row_floats * lax.rsqrt(square_sums / D + 1e-06)[None, :] * gain_here[:, None]).astype(
        jnp.bfloat16
    )
    projected = jnp.einsum(
        "jod,dr->jor",
        wqkv,
        lax.all_gather(normed, "head", axis=0, tiled=True),
        preferred_element_type=jnp.float32,
    )
    heads_here = local // HD
    projected = projected.reshape(3, heads_here, HD, rows_here)
    places = (cache_len[0] + lines).astype(jnp.float32)
    queries = rotary_columns(projected[0], places).astype(jnp.bfloat16)
    new_keys = rotary_columns(projected[1], places).astype(jnp.bfloat16)
    new_values = projected[2].astype(jnp.bfloat16)
    new_cache = jnp.stack(
        [new_keys.reshape(local, rows_here), new_values.reshape(local, rows_here)], axis=0
    )
    block_len = BS
    owned = pcache.shape[2] // block_len
    paged = pcache.reshape(2, local, owned, block_len)
    requests = block_table.shape[0]
    table_width = block_table.shape[1]
    slots_each = table_width // devices
    block_ids = here * owned + jnp.arange(owned, dtype=jnp.int32)
    matches = block_table[None, :, :] == block_ids[:, None, None]
    found = jnp.any(matches, axis=2)
    in_use = jnp.any(found, axis=1)
    owner = jnp.sum(jnp.where(found, jnp.arange(requests, dtype=jnp.int32)[None, :], 0), axis=1)
    logical = jnp.sum(
        jnp.where(matches, jnp.arange(table_width, dtype=jnp.int32)[None, None, :], 0), axis=(1, 2)
    )
    counter = jnp.arange(owned, dtype=jnp.int32)
    earlier = (
        (owner[:, None] == owner[None, :]) & in_use[None, :] & (counter[None, :] < counter[:, None])
    )
    standing = jnp.sum(earlier.astype(jnp.int32), axis=1)
    within_block = jnp.arange(block_len, dtype=jnp.int32)
    block_rows = min(rows_here, 512)
    count_blocks = rows_here // block_rows
    scale = HD ** (-0.5)
    query_blocks = jnp.transpose(
        queries.reshape(heads_here, HD, count_blocks, block_rows), (2, 0, 1, 3)
    )
    first_rows = jnp.arange(count_blocks, dtype=jnp.int32) * block_rows
    destination = owner * slots_each + standing
    routing = (destination[None, :] == jnp.arange(table_width, dtype=jnp.int32)[:, None]) & in_use[
        None, :
    ]
    outgoing = jnp.einsum(
        "wo,cfob->cfwb", routing.astype(jnp.bfloat16), paged, preferred_element_type=jnp.float32
    ).astype(jnp.bfloat16)
    outgoing = outgoing.reshape(2, local, table_width * block_len)
    labels = jnp.sum(jnp.where(routing, logical[None, :] + 1, 0), axis=1) - 1
    labels = labels.reshape(1, 1, table_width)
    blocks_in, labels_in = (
        lax.all_to_all(outgoing, "blk", split_axis=2, concat_axis=2, tiled=True),
        lax.all_to_all(labels, "blk", split_axis=2, concat_axis=2, tiled=True),
    )
    cached_keys = blocks_in[0].reshape(heads_here, HD, -1)
    cached_values = blocks_in[1].reshape(heads_here, HD, -1).astype(jnp.float32)
    label_flat = labels_in.reshape(-1)
    key_places = label_flat[:, None] * block_len + within_block[None, :]
    live = ((label_flat[:, None] >= 0) & (key_places < cache_len[0])).reshape(-1)
    old_mask = jnp.broadcast_to(live[None, :], (block_rows, live.shape[0]))
    new_values_f = new_values.astype(jnp.float32)

    def attend(inputs):
        query_block, first_row = inputs
        causal = (first_row + jnp.arange(block_rows, dtype=jnp.int32))[:, None] >= lines[None, :]
        old_part = softmax_part(query_block, cached_keys, cached_values, old_mask, scale)
        own_part = softmax_part(query_block, new_keys, new_values_f, causal, scale)
        return fold_softmax(old_part, own_part)

    mixed, highest, total = unblock(lax.map(attend, (query_blocks, first_rows)))
    attended = (mixed / total[:, None, :]).astype(jnp.bfloat16).reshape(local, rows_here)
    return (attended, new_cache)


def solution(mesh):
    in_specs = (
        P(None, "head", "blk"),
        P("head"),
        P(None, "head", None),
        P("blk"),
        P("head", "blk"),
        P(),
        P(None, "head", None),
        P(None, "head", "blk"),
        P(),
        P("blk"),
    )
    out_specs = (P("head", "blk"), P(None, "head", "blk"))
    return jax.shard_map(shards, mesh=mesh, in_specs=in_specs, out_specs=out_specs, check_vma=False)
```

profile of v0, /device:TPU:1, one launch (start us, length us, event | category | flops | bytes accessed | tf_op | source)
XLA Modules:
  0.0 288.2 jit_solution(1287686254156349032)
XLA Ops:
  7.2 1.1 convert_reduce_fusion
  8.3 20.3 %all-reduce = (f32[4,128]{1,0:T(4,128)S(1)}, f32[4,128]{1,0:T(4,128)S(1)}) all-reduce(f32[4,128]{1,0:T(4,128)S(1)} %get-tuple-element.23, f32[4,128]{1,0:T(4,128)S(1)} %get-tuple-element.22), channel_id=1, replica_groups=mesh['head'=8,'blk'=64] {'head'}, use_global_device_ids=true, to_apply=%region_11.12 | all-reduce | flops 1024 | bytes 8192 | tf_op jit(solution)/shard_map/psum | solution.py:67
  28.6 1.5 convolution_bitcast_fusion
  30.2 1.1 copy.49
  31.5 0.7 copy.44
  32.2 14.5 %all-to-all-start.2 = ((s32[64,1,1]{2,1,0:T(1,128)}), s32[64,1,1]{2,1,0:T(1,128)S(1)}, u32[]{:S(2)}, u32[]{:S(2)}) async-start(s32[64,1,1]{2,1,0:T(1,128)} %copy.44), calls=%async_computation.2 | async-start | bytes 65536 | tf_op jit(solution)/shard_map/all_to_all | solution.py:104
  46.8 2.4 compare_reduce_fusion
  49.2 0.2 convert_reduce_fusion.1
  49.4 1.4 fusion.8
  50.8 0.1 select_reduce_fusion
  50.9 0.7 copy.43
  51.7 3.7 %copy.38 = bf16[2,176,2048]{1,2,0:T(8,128)(2,1)} copy(bf16[2,176,2048]{2,1,0:T(8,128)(2,1)} %param.17) | data formatting | bytes 2883584 | tf_op args[7]
  55.4 13.9 %reduce-scatter.4.cloned.1.call-done = f32[176,128]{1,0:T(8,128)} async-done(((f32[1408,128]{1,0:T(8,128)}), f32[176,128]{1,0:T(8,128)}) %reduce-scatter.4.cloned.1.call-update) | async-done | bytes 90128
  69.2 1.0 copy.50
  70.2 0.1 reshape.265
  70.4 14.6 %all-to-all-start.1 = ((s32[1,1,128]{1,0,2:T(1,128)}), s32[1,1,128]{1,0,2:T(1,128)S(1)}, u32[]{:S(2)}, u32[]{:S(2)}) async-start(s32[1,1,128]{1,0,2:T(1,128)} %copy.43), calls=%async_computation.1 | async-start | bytes 131072 | tf_op jit(solution)/shard_map/all_to_all | solution.py:177
  85.0 0.3 convolution_convert_fusion.1
  85.3 0.8 reshape.266
  86.1 8.7 %all-to-all-done.1 = s32[1,1,128]{1,0,2:T(1,128)S(1)} async-done(((s32[1,1,128]{1,0,2:T(1,128)}), s32[1,1,128]{1,0,2:T(1,128)S(1)}, u32[]{:S(2)}, u32[]{:S(2)}) %all-to-all-start.1) | async-done | bytes 544 | tf_op jit(solution)/shard_map/all_to_all | solution.py:177
  94.8 4.4 %all-to-all-start.3 = ((bf16[64,4,176]{2,1,0:T(4,128)(2,1)}), bf16[64,4,176]{2,1,0:T(4,128)(2,1)S(1)}, u32[]{:S(2)}, u32[]{:S(2)}) async-start(bf16[64,4,176]{2,1,0:T(4,128)(2,1)} %reshape.266), calls=%async_computation.3 | async-start | bytes 262144 | tf_op jit(solution)/shard_map/all_to_all | solution.py:103
  99.2 4.9 %convert_bitcast_fusion = bf16[2,176,128,32]{2,1,3,0:T(8,128)(2,1)} fusion(bf16[2,176,64,32]{1,3,2,0:T(8,128)(2,1)} %bitcast.47, s32[64]{0:T(128)S(1)} %get-tuple-element.61, pred[64]{0:T(512)(128)(4,1)S(1)} %get-tuple-element.24), kind=kOutput, calls=%fused_computation.13 | convolution fusion | flops 186007552 | bytes 4325696 | tf_op jit(solution)/shard_map/wo,cfob->cfwb/dot_general | solution.py:169
  104.1 7.7 %copy.40 = bf16[2,176,128,32]{1,3,2,0:T(8,128)(2,1)} copy(bf16[2,176,128,32]{2,1,3,0:T(8,128)(2,1)} %convert_bitcast_fusion) | data formatting | bytes 5767168 | tf_op jit(solution)/shard_map/convert_element_type | solution.py:171
  111.8 10.1 %copy.41 = bf16[2,176,4096]{1,0,2:T(2,128)(2,1)} copy(bf16[2,176,4096]{1,2,0:T(8,128)(2,1)} %bitcast.46) | data formatting | bytes 5767168 | tf_op jit(solution)/shard_map/reshape | solution.py:172
  121.9 10.8 %all-to-all-start = ((bf16[2,176,4096]{1,0,2:T(2,128)(2,1)}), bf16[2,176,4096]{1,0,2:T(2,128)(2,1)}, u32[]{:S(2)}, u32[]{:S(2)}) async-start(bf16[2,176,4096]{1,0,2:T(2,128)(2,1)} %copy.41), calls=%async_computation | async-start | bytes 8388608 | tf_op jit(solution)/shard_map/all_to_all | solution.py:176
  132.7 0.8 dynamic_slice.9
  133.5 1.2 reduce.3
  134.8 0.1 and.66
  135.1 0.2 fusion.32
  135.4 0.4 multiply_reduce_fusion
  135.7 13.1 %psum.23 = f32[512]{0:T(512)S(1)} all-reduce(f32[512]{0:T(512)S(1)} %get-tuple-element.55), channel_id=1, replica_groups=mesh['head'=8,'blk'=64] {'head'}, use_global_device_ids=true, to_apply=%region_14.15 | all-reduce | flops 512 | bytes 4096 | tf_op jit(solution)/shard_map/psum | solution.py:118
  148.9 0.8 multiply_convert_fusion
  150.5 0.4 multiply_cosine_fusion
  150.9 2.4 multiply_reduce_fusion.1
  153.2 2.4 compare_reduce_fusion.2
  155.8 34.9 %all-gather.2.cloned.1.call-done = bf16[1408,512]{1,0:T(8,128)(2,1)} async-done(((bf16[176,512]{1,0:T(8,128)(2,1)}), bf16[1408,512]{1,0:T(8,128)(2,1)}) %all-gather.2.cloned.1.call-update) | async-done | bytes 1441808 | tf_op jit(solution)/shard_map/all_gather | solution.py:126
  190.7 2.8 fusion.15
  193.7 0.8 pad_maximum_fusion
  194.6 0.6 fusion.10
  195.3 1.3 copy-done.1
  196.6 0.6 fusion.11
  197.2 31.4 %all-to-all-done = bf16[2,176,4096]{1,0,2:T(2,128)(2,1)} async-done(((bf16[2,176,4096]{1,0,2:T(2,128)(2,1)}), bf16[2,176,4096]{1,0,2:T(2,128)(2,1)}, u32[]{:S(2)}, u32[]{:S(2)}) %all-to-all-start) | async-done | bytes 2883616 | tf_op jit(solution)/shard_map/all_to_all | solution.py:176
  228.6 9.8 %fusion.66 = (bf16[1,176,4096]{1,0,2:T(2,128)(2,1)}, bf16[1,176,4096]{1,0,2:T(2,128)(2,1)}) fusion(bf16[2,176,4096]{1,0,2:T(2,128)(2,1)} %all-to-all-done), kind=kLoop, calls=%fused_computation.118 | loop fusion | bytes 5767168 | tf_op jit(solution)/shard_map/slice | solution.py:180
  238.3 9.6 %copy.42 = bf16[1,176,4096]{2,1,0:T(8,128)(2,1)} copy(bf16[1,176,4096]{1,0,2:T(2,128)(2,1)} %get-tuple-element.41) | data formatting | bytes 2883584 | tf_op jit(solution)/shard_map/slice | solution.py:180
  247.9 9.8 %copy.45 = bf16[1,176,4096]{2,1,0:T(8,128)(2,1)S(1)} copy(bf16[1,176,4096]{1,0,2:T(2,128)(2,1)} %get-tuple-element.42) | data formatting | bytes 2883584 | tf_op jit(solution)/shard_map/slice | solution.py:179
  257.7 3.7 %fusion = (f32[2,512]{1,0:T(2,128)S(1)}, f32[2,512,4096]{2,1,0:T(8,128)S(1)}) fusion(pred[4096]{0:T(1024)(128)(4,1)S(1)} %and.63, bf16[2,88,4096]{2,1,0:T(8,128)(2,1)S(1)} %bitcast.48, bf16[2,44,512]{2,1,0:T(8,128)(2,1)} %copy-done.8, bf16[2,44,512]{2,1,0:T(8,128)(2,1)S(1)} %get-tuple-element.45), kind=kOutput, calls=%fused_computation.2 | convolution fusion | flops 751139840 | bytes 18407424 | tf_op jit(solution)/shard_map/while/body/eval_jaxpr/hdq,hdk->hqk/dot_general | solution.py:29
  261.5 5.1 %fusion.1 = f32[2,512]{1,0:T(2,128)S(1)} fusion(f32[2,512,4096]{2,1,0:T(8,128)S(1)} %get-tuple-element.60, f32[2,512]{1,0:T(2,128)S(1)} %get-tuple-element.59, pred[4096]{0:T(1024)(128)(4,1)S(1)} %and.63), kind=kLoop, calls=%fused_computation.3 | loop fusion | flops 20970496 | bytes 16789504 | tf_op jit(solution)/shard_map/while/body/eval_jaxpr/reduce_sum | solution.py:34
  266.6 1.5 fusion.20
  268.1 13.2 %fusion.29 = bf16[2,88,512]{2,1,0:T(8,128)(2,1)} fusion(f32[2,88,512]{2,1,0:T(8,128)S(1)} %fusion.20, bf16[2,88,4096]{2,1,0:T(8,128)(2,1)S(1)} %bitcast.51, f32[2,512,4096]{2,1,0:T(8,128)S(1)} %get-tuple-element.60, f32[2,512]{1,0:T(2,128)S(1)} %get-tuple-element.59, pred[4096]{0:T(1024)(128)(4,1)S(1)} %and.63, f32[2,512]{1,0:T(2,128)S(1)} %get-tuple-element.28, ...), kind=kOutput, calls=%fused_computation.39 | convolution fusion | flops 4446322688 | bytes 18776064 | tf_op jit(solution)/shard_map/while/body/eval_jaxpr/hqk,hdk->hdq/dot_general | solution.py:35
  (54 shorter events, 1.4 us)
Async XLA Ops:
  7.2 21.5 %copy-start = (bf16[4,176,1408]{2,1,0:T(8,128)(2,1)S(1)}, bf16[4,176,1408]{2,1,0:T(8,128)(2,1)}, u32[]{:S(2)}) copy-start(bf16[4,176,1408]{2,1,0:T(8,128)(2,1)} %param.12) | copy-start | bytes 5947396
  7.2 62.0 %reduce-scatter.4.cloned.1.call-start = ((), (), s32[]{:S(2)}) async-start(), calls=%async_computation.6 | async-start | bytes 811008
  28.6 2.7 copy-start.11
  28.6 18.1 %copy-start.9 = (s32[64,128]{1,0:T(8,128)S(1)}, s32[64,128]{1,0:T(8,128)}, u32[]{:S(2)}) copy-start(s32[64,128]{1,0:T(8,128)} %param.18) | copy-start | bytes 98308
  32.2 38.2 %all-to-all-start.2 = ((s32[64,1,1]{2,1,0:T(1,128)}), s32[64,1,1]{2,1,0:T(1,128)S(1)}, u32[]{:S(2)}, u32[]{:S(2)}) async-start(s32[64,1,1]{2,1,0:T(1,128)} %copy.44), calls=%async_computation.2 | async-start | bytes 65536 | tf_op jit(solution)/shard_map/all_to_all | solution.py:104
  70.4 24.4 %all-to-all-start.1 = ((s32[1,1,128]{1,0,2:T(1,128)}), s32[1,1,128]{1,0,2:T(1,128)S(1)}, u32[]{:S(2)}, u32[]{:S(2)}) async-start(s32[1,1,128]{1,0,2:T(1,128)} %copy.43), calls=%async_computation.1 | async-start | bytes 131072 | tf_op jit(solution)/shard_map/all_to_all | solution.py:177
  94.8 27.1 %all-to-all-start.3 = ((bf16[64,4,176]{2,1,0:T(4,128)(2,1)}), bf16[64,4,176]{2,1,0:T(4,128)(2,1)S(1)}, u32[]{:S(2)}, u32[]{:S(2)}) async-start(bf16[64,4,176]{2,1,0:T(4,128)(2,1)} %reshape.266), calls=%async_computation.3 | async-start | bytes 262144 | tf_op jit(solution)/shard_map/all_to_all | solution.py:103
  121.9 13.5 %copy-start.10 = (bf16[176,512]{1,0:T(8,128)(2,1)S(1)}, bf16[176,512]{1,0:T(8,128)(2,1)}, u32[]{:S(2)}) copy-start(bf16[176,512]{1,0:T(8,128)(2,1)} %param.14) | copy-start | bytes 540676
  121.9 106.7 %all-to-all-start = ((bf16[2,176,4096]{1,0,2:T(2,128)(2,1)}), bf16[2,176,4096]{1,0,2:T(2,128)(2,1)}, u32[]{:S(2)}, u32[]{:S(2)}) async-start(bf16[2,176,4096]{1,0,2:T(2,128)(2,1)} %copy.41), calls=%async_computation | async-start | bytes 8388608 | tf_op jit(solution)/shard_map/all_to_all | solution.py:176
  132.7 58.0 %all-gather.2.cloned.1.call-start = ((), (), s32[]{:S(2)}) async-start(), calls=%async_computation.5 | async-start | bytes 1622016 | tf_op jit(solution)/shard_map/all_gather | solution.py:126
  150.5 44.8 %copy-start.4 = (pred[512,512]{0,1:T(8,128)(4,1)}, pred[512,512]{0,1:T(8,128)(4,1)S(1)}, u32[]{:S(2)}) copy-start(pred[512,512]{0,1:T(8,128)(4,1)S(1)} %iota_compare_fusion) | copy-start | bytes 786436
  193.6 1.0 copy-start.6
  194.6 2.6 copy-start.8
  195.2 1.4 copy-start.1
  261.4 5.2 %copy-start.2 = (f32[2,512,512]{1,2,0:T(8,128)S(1)}, f32[2,512,512]{1,2,0:T(8,128)}, u32[]{:S(2)}) copy-start(f32[2,512,512]{1,2,0:T(8,128)} %copy-done.1) | copy-start | bytes 6291460
  261.5 5.2 %copy-start.5 = (pred[512,512]{0,1:T(8,128)(4,1)S(1)}, pred[512,512]{0,1:T(8,128)(4,1)}, u32[]{:S(2)}) copy-start(pred[512,512]{0,1:T(8,128)(4,1)} %copy-done.4) | copy-start | bytes 786436
  261.5 5.2 %copy-start.7 = (bf16[1,176,512]{2,1,0:T(8,128)(2,1)S(1)}, bf16[1,176,512]{2,1,0:T(8,128)(2,1)}, u32[]{:S(2)}) copy-start(bf16[1,176,512]{2,1,0:T(8,128)(2,1)} %copy-done.6) | copy-start | bytes 540676
  266.6 1.5 copy-start.3
Sparse Core Ops, SparseCore 0:
  31.5 37.7 reduce-scatter.3
  149.8 40.8 all-gather.1
where the time goes:
time: 290 us; the launch traced here: 288 us
  waiting for transfers between devices  88.9 us (31%)
  local copies, waits for them, and re-layouts  57.9 us (20%)
  starting transfers between devices  44.4 us (15%)
  blocking collectives  33.4 us (12%)
  matrix products  28.9 us (10%)
  other arithmetic  19.6 us (7%)
  between operations  15.1 us (5%)
    all_gather x1, waiting for transfers between devices, shards(): lax.all_gather(normed, 'head', axis=0, tiled=True)  34.9 us
    all_to_all x1, waiting for transfers between devices, shards(): lax.all_to_all(outgoing, 'blk', split_axis=2, concat_axis=2, tiled=True)  31.4 us
    psum x1, blocking collectives, shards(): lax.psum((jnp.sum(floats, axis=1), jnp.sum(floats * floats, axis=1)), 'he...  20.3 us
    slice x2, local copies, waits for them, and re-layouts, shards(): cached_values = blocks_in[1].reshape(heads_here, HD, -1).astype(jnp.float32)  19.4 us
    dot_general x2, matrix products, softmax_part(): jnp.einsum('hqk,hdk->hdq', expo, values, precision=lax.Precision.HIGHEST)  14.7 us
    all_to_all x1, starting transfers between devices, shards(): lax.all_to_all(labels, 'blk', split_axis=2, concat_axis=2, tiled=True)  14.6 us
    all_to_all x1, starting transfers between devices, shards(): lax.all_to_all(starts, 'blk', split_axis=0, concat_axis=0, tiled=True)  14.5 us
    unnamed x3, waiting for transfers between devices  13.9 us
  transfers between devices with their start and end apart: 6, of which 4 were waited for; matrix products, arithmetic and copies ran while one was open for 17% of the time, Pallas kernels for 0%

commit v1 on v0

--- a/solution.py
+++ b/solution.py
@@ -115,7 +115,7 @@
     covered = jnp.any(hits, axis=0)
     placed = jnp.where(covered[None, :], placed_rows, text)
     row_floats = placed.astype(jnp.float32)
-    square_sums = lax.psum(jnp.sum(row_floats * row_floats, axis=0), "head")
+    square_sums = jnp.sum(lax.all_gather(jnp.sum(row_floats * row_floats, axis=0), "head"), axis=0)
     gain_here = lax.dynamic_slice_in_dim(rms_gain, lax.axis_index("head") * local, local)
     normed = (row_floats * lax.rsqrt(square_sums / D + 1e-06)[None, :] * gain_here[:, None]).astype(
         jnp.bfloat16

time: 290 us -> 289 us (level)
  waiting for transfers between devices: 88.9 us -> 84 us
  blocking collectives: 33.4 us -> 38.3 us
    all_gather x0 -> x1, blocking collectives: none -> 18 us  [shards(): lax.all_gather(jnp.sum(row_floats * row_floats, axis=0), 'head')]
    psum x1 -> x0, blocking collectives: 13.1 us -> none  [shards(): square_sums = lax.psum(jnp.sum(row_floats * row_floats, axis=0), 'head')]
    all_to_all x1, waiting for transfers between devices: 31.4 us -> 26.8 us  [shards(): lax.all_to_all(outgoing, 'blk', split_axis=2, concat_axis=2, tiled=True)]
where the time goes in v1:
time: 289 us; the launch traced here: 288 us
  waiting for transfers between devices  84 us (29%)
  local copies, waits for them, and re-layouts  57.9 us (20%)
  starting transfers between devices  44.4 us (15%)
  blocking collectives  38.3 us (13%)
  matrix products  28.9 us (10%)
  other arithmetic  19.4 us (7%)
  between operations  15.1 us (5%)
    all_gather x1, waiting for transfers between devices, shards(): lax.all_gather(normed, 'head', axis=0, tiled=True)  34.5 us
    all_to_all x1, waiting for transfers between devices, shards(): lax.all_to_all(outgoing, 'blk', split_axis=2, concat_axis=2, tiled=True)  26.8 us
    psum x1, blocking collectives, shards(): lax.psum((jnp.sum(floats, axis=1), jnp.sum(floats * floats, axis=1)), 'he...  20.3 us
    slice x2, local copies, waits for them, and re-layouts, shards(): cached_values = blocks_in[1].reshape(heads_here, HD, -1).astype(jnp.float32)  19.4 us
    all_gather x1, blocking collectives, shards(): lax.all_gather(jnp.sum(row_floats * row_floats, axis=0), 'head')  18 us
    dot_general x2, matrix products, softmax_part(): jnp.einsum('hqk,hdk->hdq', expo, values, precision=lax.Precision.HIGHEST)  14.7 us
    all_to_all x1, starting transfers between devices, shards(): lax.all_to_all(labels, 'blk', split_axis=2, concat_axis=2, tiled=True)  14.6 us
    all_to_all x1, starting transfers between devices, shards(): lax.all_to_all(starts, 'blk', split_axis=0, concat_axis=0, tiled=True)  14.5 us
  transfers between devices with their start and end apart: 6, of which 4 were waited for; matrix products, arithmetic and copies ran while one was open for 17% of the time, Pallas kernels for 0%

profile of v1, /device:TPU:1, one launch (start us, length us, event | category | flops | bytes accessed | tf_op | source)
XLA Modules:
  0.0 287.9 jit_solution(14826711162441645813)
XLA Ops:
  7.2 1.1 convert_reduce_fusion
  8.3 20.3 %all-reduce = (f32[4,128]{1,0:T(4,128)S(1)}, f32[4,128]{1,0:T(4,128)S(1)}) all-reduce(f32[4,128]{1,0:T(4,128)S(1)} %get-tuple-element.23, f32[4,128]{1,0:T(4,128)S(1)} %get-tuple-element.22), channel_id=1, replica_groups=mesh['head'=8,'blk'=64] {'head'}, use_global_device_ids=true, to_apply=%region_11.12 | all-reduce | flops 1024 | bytes 8192 | tf_op jit(solution)/shard_map/psum | solution.py:67
  28.6 1.5 convolution_bitcast_fusion
  30.2 1.1 copy.49
  31.5 0.7 copy.44
  32.2 14.5 %all-to-all-start.2 = ((s32[64,1,1]{2,1,0:T(1,128)}), s32[64,1,1]{2,1,0:T(1,128)S(1)}, u32[]{:S(2)}, u32[]{:S(2)}) async-start(s32[64,1,1]{2,1,0:T(1,128)} %copy.44), calls=%async_computation.2 | async-start | bytes 65536 | tf_op jit(solution)/shard_map/all_to_all | solution.py:104
  46.8 2.4 compare_reduce_fusion
  49.2 0.2 convert_reduce_fusion.1
  49.4 1.4 fusion.8
  50.8 0.1 select_reduce_fusion
  50.9 0.7 copy.43
  51.7 3.7 %copy.38 = bf16[2,176,2048]{1,2,0:T(8,128)(2,1)} copy(bf16[2,176,2048]{2,1,0:T(8,128)(2,1)} %param.17) | data formatting | bytes 2883584 | tf_op args[7]
  55.4 13.9 %reduce-scatter.4.cloned.1.call-done = f32[176,128]{1,0:T(8,128)} async-done(((f32[1408,128]{1,0:T(8,128)}), f32[176,128]{1,0:T(8,128)}) %reduce-scatter.4.cloned.1.call-update) | async-done | bytes 90128
  69.2 1.0 copy.50
  70.2 0.1 reshape.269
  70.4 14.6 %all-to-all-start.1 = ((s32[1,1,128]{1,0,2:T(1,128)}), s32[1,1,128]{1,0,2:T(1,128)S(1)}, u32[]{:S(2)}, u32[]{:S(2)}) async-start(s32[1,1,128]{1,0,2:T(1,128)} %copy.43), calls=%async_computation.1 | async-start | bytes 131072 | tf_op jit(solution)/shard_map/all_to_all | solution.py:177
  85.0 0.3 convolution_convert_fusion.1
  85.3 0.8 reshape.270
  86.1 8.7 %all-to-all-done.1 = s32[1,1,128]{1,0,2:T(1,128)S(1)} async-done(((s32[1,1,128]{1,0,2:T(1,128)}), s32[1,1,128]{1,0,2:T(1,128)S(1)}, u32[]{:S(2)}, u32[]{:S(2)}) %all-to-all-start.1) | async-done | bytes 544 | tf_op jit(solution)/shard_map/all_to_all | solution.py:177
  94.8 4.4 %all-to-all-start.3 = ((bf16[64,4,176]{2,1,0:T(4,128)(2,1)}), bf16[64,4,176]{2,1,0:T(4,128)(2,1)S(1)}, u32[]{:S(2)}, u32[]{:S(2)}) async-start(bf16[64,4,176]{2,1,0:T(4,128)(2,1)} %reshape.270), calls=%async_computation.3 | async-start | bytes 262144 | tf_op jit(solution)/shard_map/all_to_all | solution.py:103
  99.2 4.9 %convert_bitcast_fusion = bf16[2,176,128,32]{2,1,3,0:T(8,128)(2,1)} fusion(bf16[2,176,64,32]{1,3,2,0:T(8,128)(2,1)} %bitcast.48, s32[64]{0:T(128)S(1)} %get-tuple-element.61, pred[64]{0:T(512)(128)(4,1)S(1)} %get-tuple-element.24), kind=kOutput, calls=%fused_computation.13 | convolution fusion | flops 186007552 | bytes 4325696 | tf_op jit(solution)/shard_map/wo,cfob->cfwb/dot_general | solution.py:169
  104.1 7.7 %copy.40 = bf16[2,176,128,32]{1,3,2,0:T(8,128)(2,1)} copy(bf16[2,176,128,32]{2,1,3,0:T(8,128)(2,1)} %convert_bitcast_fusion) | data formatting | bytes 5767168 | tf_op jit(solution)/shard_map/convert_element_type | solution.py:171
  111.8 10.1 %copy.41 = bf16[2,176,4096]{1,0,2:T(2,128)(2,1)} copy(bf16[2,176,4096]{1,2,0:T(8,128)(2,1)} %bitcast.47) | data formatting | bytes 5767168 | tf_op jit(solution)/shard_map/reshape | solution.py:172
  121.9 10.8 %all-to-all-start = ((bf16[2,176,4096]{1,0,2:T(2,128)(2,1)}), bf16[2,176,4096]{1,0,2:T(2,128)(2,1)}, u32[]{:S(2)}, u32[]{:S(2)}) async-start(bf16[2,176,4096]{1,0,2:T(2,128)(2,1)} %copy.41), calls=%async_computation | async-start | bytes 8388608 | tf_op jit(solution)/shard_map/all_to_all | solution.py:176
  132.7 0.8 dynamic_slice.9
  133.5 1.2 reduce.4
  134.8 0.1 and.66
  135.1 0.2 fusion.32
  135.4 0.4 multiply_reduce_fusion
  135.7 18.0 %all-gather.1 = f32[8,1,512]{2,1,0:T(1,128)S(1)} all-gather(f32[1,1,512]{2,1,0:T(1,128)S(1)} %bitcast.56), channel_id=2, replica_groups=mesh['head'=8,'blk'=64] {'head'}, dimensions={0}, use_global_device_ids=true | all-gather | bytes 18432 | tf_op jit(solution)/shard_map/all_gather | solution.py:118
  153.8 0.8 multiply_convert_fusion
  155.4 0.4 multiply_cosine_fusion
  155.8 2.4 multiply_reduce_fusion.1
  158.1 2.4 compare_reduce_fusion.2
  160.7 34.5 %all-gather.4.cloned.1.call-done = bf16[1408,512]{1,0:T(8,128)(2,1)} async-done(((bf16[176,512]{1,0:T(8,128)(2,1)}), bf16[1408,512]{1,0:T(8,128)(2,1)}) %all-gather.4.cloned.1.call-update) | async-done | bytes 1441808 | tf_op jit(solution)/shard_map/all_gather | solution.py:126
  195.3 2.8 fusion.15
  198.3 0.8 pad_maximum_fusion
  199.2 0.6 fusion.10
  199.8 1.3 copy-done.1
  201.1 0.6 fusion.11
  201.7 26.8 %all-to-all-done = bf16[2,176,4096]{1,0,2:T(2,128)(2,1)} async-done(((bf16[2,176,4096]{1,0,2:T(2,128)(2,1)}), bf16[2,176,4096]{1,0,2:T(2,128)(2,1)}, u32[]{:S(2)}, u32[]{:S(2)}) %all-to-all-start) | async-done | bytes 2883616 | tf_op jit(solution)/shard_map/all_to_all | solution.py:176
  228.6 9.8 %fusion.66 = (bf16[1,176,4096]{1,0,2:T(2,128)(2,1)}, bf16[1,176,4096]{1,0,2:T(2,128)(2,1)}) fusion(bf16[2,176,4096]{1,0,2:T(2,128)(2,1)} %all-to-all-done), kind=kLoop, calls=%fused_computation.118 | loop fusion | bytes 5767168 | tf_op jit(solution)/shard_map/slice | solution.py:180
  238.3 9.6 %copy.42 = bf16[1,176,4096]{2,1,0:T(8,128)(2,1)} copy(bf16[1,176,4096]{1,0,2:T(2,128)(2,1)} %get-tuple-element.41) | data formatting | bytes 2883584 | tf_op jit(solution)/shard_map/slice | solution.py:180
  247.9 9.8 %copy.45 = bf16[1,176,4096]{2,1,0:T(8,128)(2,1)S(1)} copy(bf16[1,176,4096]{1,0,2:T(2,128)(2,1)} %get-tuple-element.42) | data formatting | bytes 2883584 | tf_op jit(solution)/shard_map/slice | solution.py:179
  257.7 3.7 %fusion = (f32[2,512]{1,0:T(2,128)S(1)}, f32[2,512,4096]{2,1,0:T(8,128)S(1)}) fusion(pred[4096]{0:T(1024)(128)(4,1)S(1)} %and.63, bf16[2,88,4096]{2,1,0:T(8,128)(2,1)S(1)} %bitcast.49, bf16[2,44,512]{2,1,0:T(8,128)(2,1)} %copy-done.8, bf16[2,44,512]{2,1,0:T(8,128)(2,1)S(1)} %get-tuple-element.45), kind=kOutput, calls=%fused_computation.2 | convolution fusion | flops 751139840 | bytes 18407424 | tf_op jit(solution)/shard_map/while/body/eval_jaxpr/hdq,hdk->hqk/dot_general | solution.py:29
  261.5 4.9 %fusion.1 = f32[2,512]{1,0:T(2,128)S(1)} fusion(f32[2,512,4096]{2,1,0:T(8,128)S(1)} %get-tuple-element.60, f32[2,512]{1,0:T(2,128)S(1)} %get-tuple-element.59, pred[4096]{0:T(1024)(128)(4,1)S(1)} %and.63), kind=kLoop, calls=%fused_computation.3 | loop fusion | flops 20970496 | bytes 16789504 | tf_op jit(solution)/shard_map/while/body/eval_jaxpr/reduce_sum | solution.py:34
  266.4 1.5 fusion.20
  267.9 13.2 %fusion.29 = bf16[2,88,512]{2,1,0:T(8,128)(2,1)} fusion(f32[2,88,512]{2,1,0:T(8,128)S(1)} %fusion.20, bf16[2,88,4096]{2,1,0:T(8,128)(2,1)S(1)} %bitcast.52, f32[2,512,4096]{2,1,0:T(8,128)S(1)} %get-tuple-element.60, f32[2,512]{1,0:T(2,128)S(1)} %get-tuple-element.59, pred[4096]{0:T(1024)(128)(4,1)S(1)} %and.63, f32[2,512]{1,0:T(2,128)S(1)} %get-tuple-element.28, ...), kind=kOutput, calls=%fused_computation.39 | convolution fusion | flops 4446322688 | bytes 18776064 | tf_op jit(solution)/shard_map/while/body/eval_jaxpr/hqk,hdk->hdq/dot_general | solution.py:35
  (55 shorter events, 1.4 us)
Async XLA Ops:
  7.2 21.5 %copy-start = (bf16[4,176,1408]{2,1,0:T(8,128)(2,1)S(1)}, bf16[4,176,1408]{2,1,0:T(8,128)(2,1)}, u32[]{:S(2)}) copy-start(bf16[4,176,1408]{2,1,0:T(8,128)(2,1)} %param.12) | copy-start | bytes 5947396
  7.2 62.0 %reduce-scatter.4.cloned.1.call-start = ((), (), s32[]{:S(2)}) async-start(), calls=%async_computation.6 | async-start | bytes 811008
  28.6 2.7 copy-start.11
  28.6 18.1 %copy-start.9 = (s32[64,128]{1,0:T(8,128)S(1)}, s32[64,128]{1,0:T(8,128)}, u32[]{:S(2)}) copy-start(s32[64,128]{1,0:T(8,128)} %param.18) | copy-start | bytes 98308
  32.2 38.2 %all-to-all-start.2 = ((s32[64,1,1]{2,1,0:T(1,128)}), s32[64,1,1]{2,1,0:T(1,128)S(1)}, u32[]{:S(2)}, u32[]{:S(2)}) async-start(s32[64,1,1]{2,1,0:T(1,128)} %copy.44), calls=%async_computation.2 | async-start | bytes 65536 | tf_op jit(solution)/shard_map/all_to_all | solution.py:104
  70.4 24.4 %all-to-all-start.1 = ((s32[1,1,128]{1,0,2:T(1,128)}), s32[1,1,128]{1,0,2:T(1,128)S(1)}, u32[]{:S(2)}, u32[]{:S(2)}) async-start(s32[1,1,128]{1,0,2:T(1,128)} %copy.43), calls=%async_computation.1 | async-start | bytes 131072 | tf_op jit(solution)/shard_map/all_to_all | solution.py:177
  94.8 27.1 %all-to-all-start.3 = ((bf16[64,4,176]{2,1,0:T(4,128)(2,1)}), bf16[64,4,176]{2,1,0:T(4,128)(2,1)S(1)}, u32[]{:S(2)}, u32[]{:S(2)}) async-start(bf16[64,4,176]{2,1,0:T(4,128)(2,1)} %reshape.270), calls=%async_computation.3 | async-start | bytes 262144 | tf_op jit(solution)/shard_map/all_to_all | solution.py:103
  121.9 13.5 %copy-start.10 = (bf16[176,512]{1,0:T(8,128)(2,1)S(1)}, bf16[176,512]{1,0:T(8,128)(2,1)}, u32[]{:S(2)}) copy-start(bf16[176,512]{1,0:T(8,128)(2,1)} %param.14) | copy-start | bytes 540676
  121.9 106.7 %all-to-all-start = ((bf16[2,176,4096]{1,0,2:T(2,128)(2,1)}), bf16[2,176,4096]{1,0,2:T(2,128)(2,1)}, u32[]{:S(2)}, u32[]{:S(2)}) async-start(bf16[2,176,4096]{1,0,2:T(2,128)(2,1)} %copy.41), calls=%async_computation | async-start | bytes 8388608 | tf_op jit(solution)/shard_map/all_to_all | solution.py:176
  132.7 62.6 %all-gather.4.cloned.1.call-start = ((), (), s32[]{:S(2)}) async-start(), calls=%async_computation.5 | async-start | bytes 1622016 | tf_op jit(solution)/shard_map/all_gather | solution.py:126
  155.3 44.4 %copy-start.4 = (pred[512,512]{0,1:T(8,128)(4,1)}, pred[512,512]{0,1:T(8,128)(4,1)S(1)}, u32[]{:S(2)}) copy-start(pred[512,512]{0,1:T(8,128)(4,1)S(1)} %iota_compare_fusion) | copy-start | bytes 786436
  198.1 1.0 copy-start.6
  199.1 2.6 copy-start.8
  199.8 1.4 copy-start.1
  261.4 4.9 %copy-start.2 = (f32[2,512,512]{1,2,0:T(8,128)S(1)}, f32[2,512,512]{1,2,0:T(8,128)}, u32[]{:S(2)}) copy-start(f32[2,512,512]{1,2,0:T(8,128)} %copy-done.1) | copy-start | bytes 6291460
  261.5 4.9 %copy-start.5 = (pred[512,512]{0,1:T(8,128)(4,1)S(1)}, pred[512,512]{0,1:T(8,128)(4,1)}, u32[]{:S(2)}) copy-start(pred[512,512]{0,1:T(8,128)(4,1)} %copy-done.4) | copy-start | bytes 786436
  261.5 4.9 %copy-start.7 = (bf16[1,176,512]{2,1,0:T(8,128)(2,1)S(1)}, bf16[1,176,512]{2,1,0:T(8,128)(2,1)}, u32[]{:S(2)}) copy-start(bf16[1,176,512]{2,1,0:T(8,128)(2,1)} %copy-done.6) | copy-start | bytes 540676
  266.4 1.5 copy-start.3
Sparse Core Ops, SparseCore 0:
  31.5 37.7 reduce-scatter.3
  154.7 40.4 all-gather.3
